TPU v7x, 32 devices: a whole 2x2x4 slice. The times are simulated.
32 devices in a mesh: groups: 2 (over x), expert: 8 (over z, y), wave: 2 (over core).
Axes of the slice: x: 2, y: 2, z: 4, core: 2. Of those that a mesh axis runs over, the one named last changes fastest.
Arguments:
- hidden_rows: bfloat16 [512, 2, 2048], P(('groups', 'expert', 'wave')), parts along dimension 0, may hold values from -6 to 6
- expert_ids: int32 [512, 2, 8], P(('groups', 'expert', 'wave')), parts along dimension 0, may hold values from 0 to 15, all different within a row; in each aligned block of 32 rows (0 to 31, 32 to 63, ..., all dimensions but the last counted through in order) at most 24 rows name the same one
- route_weights: float32 [512, 2, 8], P(('groups', 'expert', 'wave')), parts along dimension 0, may hold values from 0.1 to 1
- w_gate: bfloat16 [16, 2048, 768], P('expert', None, 'wave'), may hold values from -0.125 to 0.125
- w_up: bfloat16 [16, 2048, 768], P('expert', None, 'wave'), may hold values from -0.125 to 0.125
- w_down: bfloat16 [16, 768, 2048], P('expert', 'wave'), may hold values from -0.21875 to 0.21875
- codes: int32 [512, 2, 16], P(('groups', 'expert', 'wave')), parts along dimension 0, may hold values from 0 to 1023
- owner_slot: int32 [512], P(('groups', 'expert', 'wave')), parts along dimension 0, may hold values from 0 to 255, as said below
- code_table: bfloat16 [16, 1024, 1024], P(None, 'expert'), may hold values from -1.5 to 1.5
- conv_state: bfloat16 [512, 6, 1024], P(('groups', 'expert', 'wave')), parts along dimension 0, may hold values from -6 to 6
- conv_taps: float32 [7, 1024], replicated, may hold values from -2.4 to 2.4
- conv_bias: float32 [1024], replicated, may hold values from -3 to 3
- upsample: bfloat16 [1024, 512], replicated, may hold values from -0.1875 to 0.1875
Outputs:
- moe_out: bfloat16 [512, 2, 2048], P(('groups', 'expert', 'wave')), parts along dimension 0
- waveform: bfloat16 [512, 2, 512], P(('groups', 'expert', 'wave')), parts along dimension 0
- new_state: bfloat16 [512, 6, 1024], P(('groups', 'expert', 'wave')), parts along dimension 0
There are 2 independent parts, one for each index of `groups`. A program takes and returns all parts, laid end to end along the dimension named above; an argument that names none is the same for every part. Nothing has to cross between parts.
Inputs may be any that keep to these rules, and one draw needn't show every extreme that they name: `expert_ids`: each row names 8 different experts; among the 32 rows of one device no expert is named more than 24 times, a bound that some block reaches. `owner_slot`: A permutation of the slots. Slot o lies on the device holding rows o of the decoder's arrays; a session's slot lies on a device with the same index along wave as the session's own device, so every device holds 16 slots.
All inputs are finite; a program needn't handle non-finite values.
Results may differ from a plain program's by a relative error of at most 0.012.
Values may be sent and summed in bfloat16 or wider, within the bound.
A program may use at most 64 MiB of HBM per device.

v0:
```python
import functools

import jax
import jax.numpy as jnp
from jax import lax
from jax.experimental import pallas as pl
from jax.experimental.pallas import tpu as pltpu
from jax.sharding import PartitionSpec as P

MESH = pl.DeviceIdType.MESH
BF = jnp.bfloat16
F32 = jnp.float32
RADIX = 64
LANES = 128
INNER = 2
HALVES = 2


def dot(a, b):
    return jnp.dot(a, b, preferred_element_type=F32)


def kernel(
    n_e, experts, books,
    h_ref, id_ref, rw_ref, co_ref, ow_ref, st_ref, tap_ref, bias_ref, us_ref,
    wg_ref, wu_ref, wd_ref, tab_ref,
    moe_ref, wave_ref, new_ref,
    hv, idv, rwv, cov, owv, stv, tapv, biasv, usv,
    xg, meta, wgu, wdv, tabv, mem, act, early, told, po, pn, my, ma, mz,
    fs, fy, fa, fz, fr,
    in_sem, w_sem, pws, pwr, zus, zds, yss, agr, mes, mer,
    mys, myr, mzs, mzr, fys, fyr, fzs, fzr,
):
    outer = n_e // INNER
    sessions, steps, width = hv.shape
    rows = sessions * steps
    channels = tab_ref.shape[1]
    local, _, units = wg_ref.shape
    ff = 2 * units
    shard = tab_ref.shape[0] // books
    wave_rows = n_e * rows
    col_rows = outer * rows
    e = lax.axis_index("expert")
    w = lax.axis_index("wave")
    z = e // INNER
    y = e % INNER
    peer = 1 - w
    ye = z * INNER + (1 - y)
    low = z < outer // 2

    def remote(src, dst, ssem, rsem, te, tw):
        return pltpu.make_async_remote_copy(
            src_ref=src, dst_ref=dst, send_sem=ssem, recv_sem=rsem,
            device_id={"expert": te, "wave": tw}, device_id_type=MESH,
        )

    barrier = pltpu.get_barrier_semaphore()

    def greet(te, tw):
        pl.semaphore_signal(barrier, inc=1, device_id={"expert": te, "wave": tw}, device_id_type=MESH)

    greet(e, peer)
    for d in range(1, n_e):
        greet((e + d) % n_e, w)

    firsts = [
        pltpu.make_async_copy(src, dst, in_sem.at[i])
        for i, (src, dst) in enumerate((
            (h_ref, hv), (id_ref, idv), (rw_ref, rwv), (co_ref, cov), (ow_ref, owv),
            (st_ref, stv), (tap_ref, tapv), (bias_ref, biasv), (us_ref, usv),
        ))
    ]
    for copy in firsts[:5]:
        copy.start()

    def gate_at(tw):
        return pl.ds(pl.multiple_of(tw * units, LANES), units)

    def up_at(tw):
        return pl.ds(pl.multiple_of(ff + tw * units, LANES), units)

    def down_at(j, tw):
        return pl.ds(pl.multiple_of(j * ff + tw * units, LANES), units)

    def weights(tw):
        pairs = []
        for j in range(local):
            pairs.append((wg_ref.at[j], wgu.at[j, :, gate_at(tw)]))
            pairs.append((wu_ref.at[j], wgu.at[j, :, up_at(tw)]))
        for j in range(local):
            pairs.append((wd_ref.at[pl.ds(j * units, units), :], wdv.at[down_at(j, tw), :]))
        return pairs

    loads = [
        pltpu.make_async_copy(src, dst, w_sem.at[i]) for i, (src, dst) in enumerate(weights(w))
    ]
    table = pltpu.make_async_copy(tab_ref, tabv, w_sem.at[3 * local])
    gives = [
        remote(src, dst, pws.at[i], pwr.at[i], e, peer) for i, (src, dst) in enumerate(weights(w))
    ]
    takes = [
        remote(src, dst, pws.at[i], pwr.at[i], e, peer) for i, (src, dst) in enumerate(weights(peer))
    ]

    half = rows // HALVES

    def at(rel, zo, p):
        return pl.ds(pl.multiple_of((rel * outer + zo) * rows + p * half, half), half)

    def agsem(rel, zo, p):
        return agr.at[(rel * outer + zo) * HALVES + p]

    def up(zo, p):
        s = xg.at[at(0, zo, p), :]
        return remote(s, s, zus.at[zo * HALVES + p], agsem(0, zo, p), (z + 1) * INNER + y, w)

    def down(zo, p):
        s = xg.at[at(0, zo, p), :]
        return remote(s, s, zds.at[zo * HALVES + p], agsem(0, zo, p), (z - 1) * INNER + y, w)

    def across(zo, p):
        return remote(
            xg.at[at(0, zo, p), :], xg.at[at(1, zo, p), :], yss.at[zo * HALVES + p], agsem(1, zo, p), ye, w
        )

    def arrived(rel, zo, p):
        s = xg.at[at(rel, zo, p), :]
        remote(s, s, yss.at[0], agsem(rel, zo, p), ye, w).wait_recv()

    def meta_at(te, se):
        rel = (te % INNER + se % INNER) % 2
        return pl.ds(pl.multiple_of((rel * outer + se // INNER) * rows, rows), rows)

    def tell(d):
        te = (e + d) % n_e
        return remote(
            meta.at[meta_at(e, e), :], meta.at[meta_at(te, e), :], mes.at[d - 1], mer.at[d - 1], te, w
        )

    def told_by(d):
        se = (e - d + n_e) % n_e
        s = meta.at[meta_at(e, se), :]
        return remote(s, s, mes.at[d - 1], mer.at[d - 1], se, w)

    firsts[0].wait()
    hid = hv[...]
    mine_at = pl.multiple_of(z * rows, rows)
    for t in range(steps):
        xg[pl.ds(mine_at + t * sessions, sessions), :] = hid[:, t, :]
    for copy in firsts[5:]:
        copy.start()
    table.start()
    for load in loads:
        load.start()
    pl.semaphore_wait(barrier, n_e)

    for p in range(HALVES):
        @pl.when(z + 1 < outer)
        def _():
            up(z, p).start()

        @pl.when(z > 0)
        def _():
            down(z, p).start()

        across(z, p).start()
    for give in gives:
        give.start()

    lanes = meta.shape[1]
    code_at = 2 * experts
    dest_at = code_at + 2 * books
    lane_i = lax.broadcasted_iota(jnp.int32, (sessions, lanes), 1)
    eye = lax.broadcasted_iota(jnp.int32, (sessions, sessions), 0) == lax.broadcasted_iota(
        jnp.int32, (sessions, sessions), 1
    )
    lane_f = lane_i.astype(F32)

    def column(row):
        square = jnp.broadcast_to(row.astype(F32), (sessions, sessions))
        return jnp.sum(jnp.where(eye, square, 0.0), axis=1, keepdims=True)

    for copy in firsts[1:5]:
        copy.wait()
    owner = column(owv[...])
    holder = jnp.floor((owner + 0.5) / sessions)
    within = owner - holder * sessions
    holder = jnp.floor((holder + 0.5) / 2)
    for t in range(steps):
        co = cov[:, t, :].astype(F32)
        both = jnp.zeros((sessions, lanes), F32)
        for k in range(idv.shape[1]):
            named = column(idv[t, k:k + 1, :])
            both += jnp.where(
                (named == lane_f) | (named + experts == lane_f), column(rwv[t, k:k + 1, :]), 0.0
            )
        high = both.astype(BF).astype(F32)
        extra = jnp.where(lane_i < experts, high, both - high)
        extra = jnp.where(lane_i < code_at, extra, 0.0)
        for q in range(books):
            c = co[:, q:q + 1]
            top = jnp.floor((c + 0.5) / RADIX)
            extra = jnp.where(lane_i == code_at + q, top, extra)
            extra = jnp.where(lane_i == code_at + books + q, c - top * RADIX, extra)
        dest = holder * rows + t * sessions + within
        top = jnp.floor((dest + 0.5) / RADIX)
        extra = jnp.where(lane_i == dest_at, top, extra)
        extra = jnp.where(lane_i == dest_at + 1, dest - top * RADIX, extra)
        meta[pl.ds(mine_at + t * sessions, sessions), :] = extra.astype(BF)
    for d in range(1, n_e):
        tell(d).start()

    for copy in firsts[5:]:
        copy.wait()
    state_len = stv.shape[0]
    taps = tapv.shape[0]

    def before():
        for t in range(steps):
            total = jnp.broadcast_to(biasv[...], (sessions, channels))
            for j in range(t + 1, taps):
                total += tapv[j:j + 1, :] * stv[state_len + t - j].astype(F32)
            early[t * sessions:(t + 1) * sessions, :] = total
        for i in range(state_len - steps):
            new_ref[i] = stv[i + steps]

    def forward(step):
        for p in range(HALVES):
            @pl.when(z - step >= 0)
            def _():
                zo = z - step
                arrived(0, zo, p)

                @pl.when(z + 1 < outer)
                def _():
                    up(zo, p).start()

                across(zo, p).start()

            @pl.when(z + step < outer)
            def _():
                zo = z + step
                arrived(0, zo, p)

                @pl.when(z > 0)
                def _():
                    down(zo, p).start()

                across(zo, p).start()

    src = lax.broadcasted_iota(jnp.int32, (lanes, LANES), 0)
    col = lax.broadcasted_iota(jnp.int32, (lanes, LANES), 1)

    def learn():
        for d in range(1, n_e):
            told_by(d).wait_recv()
        is_code = col < books
        pick = jnp.where(is_code & (src == code_at + col), float(RADIX), 0.0)
        pick += jnp.where(is_code & (src == code_at + books + col), 1.0, 0.0)
        pick += jnp.where((col == books) & (src == dest_at), float(RADIX), 0.0)
        pick += jnp.where((col == books) & (src == dest_at + 1), 1.0, 0.0)
        own = e * local + col - (books + 1)
        is_weight = (col > books) & (col <= books + local)
        pick += jnp.where(is_weight & ((src == own) | (src == own + experts)), 1.0, 0.0)
        told[...] = dot(meta[...], pick.astype(BF))
        lane = lax.broadcasted_iota(jnp.int32, (wave_rows, shard), 1).astype(F32)
        first = (e * shard).astype(F32)
        for q in range(books):
            mem[:, q * shard:(q + 1) * shard] = jnp.where(
                told[:, q:q + 1] - first == lane, 1.0, 0.0
            ).astype(BF)

    def embed():
        place = lax.broadcasted_iota(jnp.int32, (wave_rows, wave_rows), 1).astype(F32)
        order = jnp.where(told[:, books:books + 1] == place, 1.0, 0.0).astype(BF)
        table.wait()
        f_tile = min(channels, 512)

        @pl.loop(0, channels // f_tile)
        def _(n):
            cols = pl.ds(pl.multiple_of(n * f_tile, f_tile), f_tile)
            part = dot(mem[...], tabv[:, cols]).astype(BF)
            fs[:, cols] = lax.dot_general(
                order, part, (((0,), (0,)), ((), ())), preferred_element_type=F32
            ).astype(BF)

    def goal(k):
        if k == outer - 1:
            return z
        down_from = outer - 1 - k
        down_from = down_from - (down_from <= z).astype(jnp.int32)
        up_from = k + (k >= z).astype(jnp.int32)
        return jnp.where(low, down_from, up_from)

    def block(zo, yo):
        return pl.ds(pl.multiple_of((zo * INNER + yo) * rows, rows), rows)

    def zrows(zo):
        return pl.ds(pl.multiple_of(zo * rows, rows), rows)

    def hop(zo):
        return (zo - z + outer) % outer - 1

    def fy_copy(zo):
        return remote(fs.at[block(zo, 1 - y), :], fy.at[zrows(zo), :], fys.at[zo], fyr.at[zo], ye, w)

    def fz_copy(zo):
        d = hop(zo)
        return remote(fa.at[zrows(zo), :], fz.at[zrows(d), :], fzs.at[d], fzr.at[d], zo * INNER + y, w)

    def fz_got(d):
        s = fz.at[zrows(d), :]
        return remote(s, s, fzs.at[d], fzr.at[d], ye, w)

    part_cols = width // HALVES

    def cols_of(p):
        return pl.ds(p * part_cols, part_cols)

    def my_copy(zo, p):
        i = zo * HALVES + p
        return remote(
            pn.at[zrows(zo), cols_of(p)], my.at[zrows(zo), cols_of(p)], mys.at[i], myr.at[i], ye, w
        )

    def mz_copy(zo, p):
        d = hop(zo)
        i = d * HALVES + p
        return remote(
            ma.at[zrows(zo), cols_of(p)], mz.at[zrows(d), cols_of(p)], mzs.at[i], mzr.at[i], zo * INNER + y, w
        )

    def mz_got(d, p):
        i = d * HALVES + p
        s = mz.at[zrows(d), cols_of(p)]
        return remote(s, s, mzs.at[i], mzr.at[i], ye, w)

    rc = min(col_rows, 128)

    def looped(count, body):
        if count == 1:
            body(0)
        else:
            pl.loop(0, count)(body)

    def hidden(rel):
        def piece(i):
            here = pl.ds(pl.multiple_of(rel * col_rows + i * rc, rc), rc)
            there = pl.ds(pl.multiple_of(i * rc, rc), rc)
            x = xg[here, :]
            tile = ff // 3 if ff % (3 * LANES) == 0 else ff
            for j in range(local):
                weight = told[here, books + 1 + j:books + 2 + j]
                for n in range(0, ff, tile):
                    g = dot(x, wgu[j, :, n:n + tile])
                    u = dot(x, wgu[j, :, ff + n:ff + n + tile])
                    a = g / (1.0 + jnp.exp(-g)) * u * weight
                    act[there, j * ff + n:j * ff + n + tile] = a.astype(BF)

        looped(col_rows // rc, piece)

    def project(dst, p):
        def piece(i):
            there = pl.ds(pl.multiple_of(i * rc, rc), rc)
            tile = min(part_cols, 512)
            for n in range(p * part_cols, (p + 1) * part_cols, tile):
                dst[there, n:n + tile] = dot(act[there, :], wdv[:, n:n + tile]).astype(BF)

        looped(col_rows // rc, piece)

    before()
    for step in range(1, outer):
        forward(step)
        if step == 1:
            learn()
        if step == min(2, outer - 1):
            embed()
    for k in range(outer):
        fy_copy(goal(k)).start()

    for load in loads:
        load.wait()
    for take in takes:
        take.wait_recv()
    hidden(0)
    for p in range(HALVES):
        project(po, p)
    for zo in range(outer):
        for p in range(HALVES):
            arrived(1, zo, p)
    hidden(1)
    for p in range(HALVES):
        project(pn, p)
        for k in range(outer - 1):
            my_copy(goal(k), p).start()
    for p in range(HALVES):
        my_copy(z, p).start()

    for k in range(outer):
        zo = goal(k)
        total = fs[block(zo, y), :].astype(F32)
        fy_copy(zo).wait_recv()
        total += fy[zrows(zo), :].astype(F32)
        if k < outer - 1:
            fa[zrows(zo), :] = total.astype(BF)
            fz_copy(zo).start()
        else:
            fr[...] = total

    def pass_on(p):
        for k in range(outer - 1):
            zo = goal(k)
            my_copy(zo, p).wait_recv()
            ma[zrows(zo), cols_of(p)] = (
                po[zrows(zo), cols_of(p)].astype(F32) + my[zrows(zo), cols_of(p)].astype(F32)
            ).astype(BF)
            mz_copy(zo, p).start()

    def finish_frames():
        for d in range(outer - 1):
            fz_got(d).wait_recv()
            fr[...] += fz[zrows(d), :].astype(F32)
        got = [fr[t * sessions:(t + 1) * sessions, :] for t in range(steps)]
        decoded = []
        for t in range(steps):
            total = early[t * sessions:(t + 1) * sessions, :]
            for j in range(t + 1):
                total += tapv[j:j + 1, :] * got[t - j]
            decoded.append(jax.nn.gelu(total).astype(BF))
            new_ref[state_len - steps + t] = got[t].astype(BF)
        samples = dot(jnp.concatenate(decoded, axis=0), usv[...]).astype(BF)
        for t in range(steps):
            wave_ref[:, t, :] = samples[t * sessions:(t + 1) * sessions]

    pass_on(0)
    finish_frames()
    for p in range(1, HALVES):
        pass_on(p)
    for p in range(HALVES):
        my_copy(z, p).wait_recv()
        mine = po[zrows(z), cols_of(p)].astype(F32) + my[zrows(z), cols_of(p)].astype(F32)
        for d in range(outer - 1):
            mz_got(d, p).wait_recv()
            mine += mz[zrows(d), cols_of(p)].astype(F32)
        for t in range(steps):
            moe_ref[:, t, p * part_cols:(p + 1) * part_cols] = mine[t * sessions:(t + 1) * sessions].astype(BF)

    for give in gives:
        give.wait_send()
    for d in range(1, n_e):
        tell(d).wait_send()
    for zo in range(outer):
        for p in range(HALVES):
            @pl.when((z + 1 < outer) & (zo <= z))
            def _():
                up(zo, p).wait_send()

            @pl.when((z > 0) & (zo >= z))
            def _():
                down(zo, p).wait_send()

            across(zo, p).wait_send()
            my_copy(zo, p).wait_send()
        fy_copy(zo).wait_send()
    for k in range(outer - 1):
        zo = goal(k)
        fz_copy(zo).wait_send()
        for p in range(HALVES):
            mz_copy(zo, p).wait_send()


def hand_over(a_ref, b_ref, c_ref, a_out, b_out, c_out):
    a_out[...] = a_ref[...]
    b_out[...] = b_ref[...]
    c_out[...] = c_ref[...]


def exchange(args, w_gate, w_up, w_down, table, experts, books):
    n_e = lax.axis_size("expert")
    outer = n_e // INNER
    sessions, steps, width = args[0].shape
    rows = sessions * steps
    used = 2 * experts + 2 * books + 2
    lanes = used + -used % LANES
    local, _, units = w_gate.shape
    ff = 2 * units
    channels = table.shape[1]
    wave_rows = n_e * rows
    col_rows = outer * rows
    vm = pltpu.VMEM
    dma = lambda *s: pltpu.SemaphoreType.DMA(s)
    hops = outer - 1
    scratch = [vm(a.shape, a.dtype) for a in args] + [
        vm((wave_rows, width), BF),
        vm((wave_rows, lanes), BF),
        vm((local, width, 2 * ff), BF),
        vm((local * ff, width), BF),
        vm(table.shape, BF),
        vm((wave_rows, table.shape[0]), BF),
        vm((col_rows, local * ff), BF),
        vm((rows, channels), F32),
        vm((wave_rows, LANES), F32),
        vm((col_rows, width), BF),
        vm((col_rows, width), BF),
        vm((col_rows, width), BF),
        vm((col_rows, width), BF),
        vm((hops * rows, width), BF),
        vm((wave_rows, channels), BF),
        vm((col_rows, channels), BF),
        vm((col_rows, channels), BF),
        vm((hops * rows, channels), BF),
        vm((rows, channels), F32),
        dma(len(args)), dma(3 * local + 1), dma(3 * local), dma(3 * local),
        dma(outer * HALVES), dma(outer * HALVES), dma(outer * HALVES), dma(n_e * HALVES),
        dma(n_e - 1), dma(n_e - 1),
        dma(outer * HALVES), dma(outer * HALVES), dma(hops * HALVES), dma(hops * HALVES),
        dma(outer), dma(outer), dma(hops), dma(hops),
    ]
    any_spec = pl.BlockSpec(memory_space=pl.ANY)
    vm_spec = pl.BlockSpec(memory_space=pltpu.VMEM)
    return pl.pallas_call(
        functools.partial(kernel, n_e, experts, books),
        out_shape=(
            jax.ShapeDtypeStruct((sessions, steps, width), BF),
            jax.ShapeDtypeStruct((sessions, steps, args[8].shape[1]), BF),
            jax.ShapeDtypeStruct(args[5].shape, BF),
        ),
        in_specs=[any_spec] * (len(args) + 4),
        out_specs=(vm_spec, vm_spec, vm_spec),
        scratch_shapes=scratch,
        compiler_params=pltpu.CompilerParams(
            collective_id=0, has_side_effects=True, vmem_limit_bytes=60 * 1024 * 1024
        ),
    )(*args, w_gate, w_up, w_down, table)


def per_device(
    hidden_rows, expert_ids, route_weights, w_gate, w_up, w_down,
    codes, owner_slot, code_table, conv_state, conv_taps, conv_bias, upsample,
):
    n_e = lax.axis_size("expert")
    width = hidden_rows.shape[2]
    experts = n_e * w_gate.shape[0]
    books, shard, channels = code_table.shape
    results = exchange(
        (
            hidden_rows, expert_ids.transpose(1, 2, 0), route_weights.transpose(1, 2, 0), codes,
            owner_slot.reshape(1, -1), conv_state.transpose(1, 0, 2), conv_taps, conv_bias.reshape(1, -1), upsample,
        ),
        w_gate, w_up, w_down.reshape(-1, width), code_table.reshape(books * shard, channels),
        experts, books,
    )
    vm_spec = pl.BlockSpec(memory_space=pltpu.VMEM)
    moe, samples, carried = pl.pallas_call(
        hand_over,
        out_shape=tuple(jax.ShapeDtypeStruct(r.shape, r.dtype) for r in results),
        in_specs=[vm_spec] * 3,
        out_specs=(vm_spec,) * 3,
    )(*results)
    return moe, samples, carried.transpose(1, 0, 2)


def solution(mesh):
    rows = P(("groups", "expert", "wave"), None, None)
    placed = (
        rows, rows, rows,
        P("expert", None, "wave"), P("expert", None, "wave"), P("expert", "wave", None),
        rows, P(("groups", "expert", "wave")), P(None, "expert", None), rows, P(), P(), P(),
    )
    return jax.shard_map(
        per_device, mesh=mesh, in_specs=placed, out_specs=(rows, rows, rows), check_vma=False
    )
```

profile of v0, /device:TPU:0, one launch (start us, length us, event | category | flops | bytes accessed | tf_op | source)
XLA Modules:
  0.0 47.2 jit_solution(3154755277037217319)
XLA Ops:
  0.6 44.8 %shard_map.148 = (bf16[16,2,2048]{2,1,0:T(2,128)(2,1)}, bf16[16,2,512]{2,1,0:T(2,128)(2,1)}, bf16[6,16,1024]{2,1,0:T(8,128)(2,1)}) custom-call(bf16[16,2,2048]{2,1,0:T(2,128)(2,1)} %h_ref.1, s32[2,8,16]{2,1,0:T(8,128)} %bitcast.11, f32[2,8,16]{2,1,0:T(8,128)} %bitcast.12, s32[16,2,16]{2,1,0:T(2,128)} %co_ref.1, s32[1,16]{1,0:T(1,128)} %bitcast.14, ...), custom_call_target="tpu_custom_call" | custom-call | tf_op jit(solution)/shard_map/pallas_call | solution.py:521
  45.5 1.7 %shard_map.149 = (bf16[16,2,2048]{2,1,0:T(2,128)(2,1)}, bf16[16,2,512]{2,1,0:T(2,128)(2,1)}, bf16[6,16,1024]{2,1,0:T(8,128)(2,1)}) custom-call(bf16[16,2,2048]{2,1,0:T(2,128)(2,1)} %get-tuple-element.9.a_ref, bf16[16,2,512]{2,1,0:T(2,128)(2,1)} %get-tuple-element.10.b_ref, bf16[6,16,1024]{2,1,0:T(8,128)(2,1)} %get-tuple-element.11.c_ref), custom_call_target="tpu_custom_call" | custom-call | tf_op jit(solution)/shard_map/pallas_call | solution.py:554
where the time goes:
time: 47.4 us; the launch traced here: 47.2 us
  Pallas kernels  46.6 us (98%)
  between operations  0.64 us (1%)
    pallas_call x1, Pallas kernels, exchange(): pl.pallas_call(functools.partial(kernel, n_e, experts, books), out_shape=...  44.8 us
    pallas_call x1, Pallas kernels, per_device(): pl.pallas_call(hand_over, out_shape=tuple((jax.ShapeDtypeStruct(r.shape,...  1.74 us

commit v1 on v0

--- a/solution.py
+++ b/solution.py
@@ -26,10 +26,10 @@
     wg_ref, wu_ref, wd_ref, tab_ref,
     moe_ref, wave_ref, new_ref,
     hv, idv, rwv, cov, owv, stv, tapv, biasv, usv,
-    xg, meta, wgu, wdv, tabv, mem, act, early, told, po, pn, my, ma, mz,
+    xg, meta, wgu, wdv, tabv, mem, act, early, told, po, pn, my, ma, mz, mine,
     fs, fy, fa, fz, fr,
     in_sem, w_sem, pws, pwr, zus, zds, yss, agr, mes, mer,
-    mys, myr, mzs, mzr, fys, fyr, fzs, fzr,
+    mys, myr, mzs, mzr, fys, fyr, fzs, fzr, below, above, aside,
 ):
     outer = n_e // INNER
     sessions, steps, width = hv.shape
@@ -60,8 +60,15 @@
         pl.semaphore_signal(barrier, inc=1, device_id={"expert": te, "wave": tw}, device_id_type=MESH)
 
     greet(e, peer)
-    for d in range(1, n_e):
-        greet((e + d) % n_e, w)
+    greet(ye, w)
+
+    @pl.when(z > 0)
+    def _():
+        greet(e - INNER, w)
+
+    @pl.when(z < outer - 1)
+    def _():
+        greet(e + INNER, w)
 
     firsts = [
         pltpu.make_async_copy(src, dst, in_sem.at[i])
@@ -152,7 +159,7 @@
     table.start()
     for load in loads:
         load.start()
-    pl.semaphore_wait(barrier, n_e)
+    pl.semaphore_wait(barrier, 2 + (z > 0).astype(jnp.int32) + (z < outer - 1).astype(jnp.int32))
 
     for p in range(HALVES):
         @pl.when(z + 1 < outer)
@@ -168,45 +175,73 @@
         give.start()
 
     lanes = meta.shape[1]
-    code_at = 2 * experts
-    dest_at = code_at + 2 * books
-    lane_i = lax.broadcasted_iota(jnp.int32, (sessions, lanes), 1)
-    eye = lax.broadcasted_iota(jnp.int32, (sessions, sessions), 0) == lax.broadcasted_iota(
-        jnp.int32, (sessions, sessions), 1
-    )
-    lane_f = lane_i.astype(F32)
-
-    def column(row):
-        square = jnp.broadcast_to(row.astype(F32), (sessions, sessions))
-        return jnp.sum(jnp.where(eye, square, 0.0), axis=1, keepdims=True)
+    dest_at = 2 * experts
+    code_at = dest_at + 8
+
+    def placed(count, start):
+        here = lax.broadcasted_iota(jnp.int32, (count, lanes), 0)
+        there = lax.broadcasted_iota(jnp.int32, (count, lanes), 1)
+        return jnp.where(here + start == there, 1.0, 0.0).astype(BF)
 
     for copy in firsts[1:5]:
         copy.wait()
-    owner = column(owv[...])
+    owner = owv[...].astype(F32)
     holder = jnp.floor((owner + 0.5) / sessions)
     within = owner - holder * sessions
     holder = jnp.floor((holder + 0.5) / 2)
+    expert_i = lax.broadcasted_iota(jnp.int32, (experts, sessions), 0)
+    digit = lax.broadcasted_iota(jnp.int32, (8, sessions), 0)
     for t in range(steps):
-        co = cov[:, t, :].astype(F32)
-        both = jnp.zeros((sessions, lanes), F32)
+        both = jnp.zeros((experts, sessions), F32)
         for k in range(idv.shape[1]):
-            named = column(idv[t, k:k + 1, :])
-            both += jnp.where(
-                (named == lane_f) | (named + experts == lane_f), column(rwv[t, k:k + 1, :]), 0.0
-            )
+            both += jnp.where(expert_i == idv[t, k:k + 1, :], rwv[t, k:k + 1, :], 0.0)
         high = both.astype(BF).astype(F32)
-        extra = jnp.where(lane_i < experts, high, both - high)
-        extra = jnp.where(lane_i < code_at, extra, 0.0)
-        for q in range(books):
-            c = co[:, q:q + 1]
-            top = jnp.floor((c + 0.5) / RADIX)
-            extra = jnp.where(lane_i == code_at + q, top, extra)
-            extra = jnp.where(lane_i == code_at + books + q, c - top * RADIX, extra)
         dest = holder * rows + t * sessions + within
         top = jnp.floor((dest + 0.5) / RADIX)
-        extra = jnp.where(lane_i == dest_at, top, extra)
-        extra = jnp.where(lane_i == dest_at + 1, dest - top * RADIX, extra)
+        digits = jnp.where(digit == 0, top, jnp.where(digit == 1, dest - top * RADIX, 0.0))
+        upright = jnp.concatenate([high, both - high, digits], axis=0).astype(BF)
+        extra = lax.dot_general(
+            upright, placed(code_at, 0), (((0,), (0,)), ((), ())), preferred_element_type=F32
+        )
+        co = cov[:, t, :].astype(F32)
+        top = jnp.floor((co + 0.5) / RADIX)
+        extra += dot(top.astype(BF), placed(books, code_at))
+        extra += dot((co - top * RADIX).astype(BF), placed(books, code_at + books))
         meta[pl.ds(mine_at + t * sessions, sessions), :] = extra.astype(BF)
+
+    def signal(sem, te):
+        pl.semaphore_signal(sem, inc=1, device_id={"expert": te, "wave": w}, device_id_type=MESH)
+
+    def upward():
+        @pl.when(z > 0)
+        def _():
+            pl.semaphore_wait(below, 1)
+
+        @pl.when(z < outer - 1)
+        def _():
+            signal(below, e + INNER)
+
+    def downward():
+        @pl.when(z < outer - 1)
+        def _():
+            pl.semaphore_wait(above, 1)
+
+        @pl.when(z > 0)
+        def _():
+            signal(above, e - INNER)
+
+    @pl.when(low)
+    def _():
+        upward()
+        downward()
+
+    @pl.when(jnp.logical_not(low))
+    def _():
+        downward()
+        upward()
+
+    signal(aside, ye)
+    pl.semaphore_wait(aside, 1)
     for d in range(1, n_e):
         tell(d).start()
 
@@ -324,16 +359,15 @@
         )
 
     def mz_copy(zo, p):
-        d = hop(zo)
-        i = d * HALVES + p
+        there = (z - zo + outer) % outer
         return remote(
-            ma.at[zrows(zo), cols_of(p)], mz.at[zrows(d), cols_of(p)], mzs.at[i], mzr.at[i], zo * INNER + y, w
+            ma.at[zrows(zo), cols_of(p)], mz.at[zrows(there), cols_of(p)],
+            mzs.at[zo * HALVES + p], mzr.at[there * HALVES + p], zo * INNER + y, w,
         )
 
-    def mz_got(d, p):
-        i = d * HALVES + p
-        s = mz.at[zrows(d), cols_of(p)]
-        return remote(s, s, mzs.at[i], mzr.at[i], ye, w)
+    def mz_got(there, p):
+        s = mz.at[zrows(there), cols_of(p)]
+        return remote(s, s, mzs.at[0], mzr.at[there * HALVES + p], ye, w)
 
     rc = min(col_rows, 128)
 
@@ -343,30 +377,44 @@
         else:
             pl.loop(0, count)(body)
 
-    def hidden(rel):
+    def ready(i):
+        loads[i].wait()
+        takes[i].wait_recv()
+
+    def hidden(rel, j):
+        def piece(i):
+            here = pl.ds(pl.multiple_of(rel * col_rows + i * rc, rc), rc)
+            x = xg[here, :]
+            weight = told[here, books + 1 + j:books + 2 + j]
+            tile = ff // 3 if ff % (3 * LANES) == 0 else ff
+            for n in range(0, ff, tile):
+                g = dot(x, wgu[j, :, n:n + tile])
+                u = dot(x, wgu[j, :, ff + n:ff + n + tile])
+                a = g / (1.0 + jnp.exp(-g)) * u * weight
+                act[here, j * ff + n:j * ff + n + tile] = a.astype(BF)
+
+        looped(col_rows // rc, piece)
+
+    def project(rel, dst, p):
         def piece(i):
             here = pl.ds(pl.multiple_of(rel * col_rows + i * rc, rc), rc)
             there = pl.ds(pl.multiple_of(i * rc, rc), rc)
-            x = xg[here, :]
-            tile = ff // 3 if ff % (3 * LANES) == 0 else ff
-            for j in range(local):
-                weight = told[here, books + 1 + j:books + 2 + j]
-                for n in range(0, ff, tile):
-                    g = dot(x, wgu[j, :, n:n + tile])
-                    u = dot(x, wgu[j, :, ff + n:ff + n + tile])
-                    a = g / (1.0 + jnp.exp(-g)) * u * weight
-                    act[there, j * ff + n:j * ff + n + tile] = a.astype(BF)
-
-        looped(col_rows // rc, piece)
-
-    def project(dst, p):
-        def piece(i):
-            there = pl.ds(pl.multiple_of(i * rc, rc), rc)
             tile = min(part_cols, 512)
             for n in range(p * part_cols, (p + 1) * part_cols, tile):
-                dst[there, n:n + tile] = dot(act[there, :], wdv[:, n:n + tile]).astype(BF)
+                dst[there, n:n + tile] = dot(act[here, :], wdv[:, n:n + tile]).astype(BF)
 
         looped(col_rows // rc, piece)
+
+    def frames_on(k):
+        zo = goal(k)
+        total = fs[block(zo, y), :].astype(F32)
+        fy_copy(zo).wait_recv()
+        total += fy[zrows(zo), :].astype(F32)
+        if k < outer - 1:
+            fa[zrows(zo), :] = total.astype(BF)
+            fz_copy(zo).start()
+        else:
+            fr[...] = total
 
     before()
     for step in range(1, outer):
@@ -378,42 +426,36 @@
     for k in range(outer):
         fy_copy(goal(k)).start()
 
-    for load in loads:
-        load.wait()
-    for take in takes:
-        take.wait_recv()
-    hidden(0)
-    for p in range(HALVES):
-        project(po, p)
+    for j in range(local):
+        ready(2 * j)
+        ready(2 * j + 1)
+        hidden(0, j)
     for zo in range(outer):
         for p in range(HALVES):
             arrived(1, zo, p)
-    hidden(1)
+    for j in range(local):
+        hidden(1, j)
+        if j < outer - 1:
+            frames_on(j)
+    for j in range(local):
+        ready(2 * local + j)
     for p in range(HALVES):
-        project(pn, p)
-        for k in range(outer - 1):
+        project(1, pn, p)
+        my_copy(goal(0), p).start()
+    for k in range(1, outer):
+        for p in range(HALVES):
             my_copy(goal(k), p).start()
+    for k in range(min(local, outer - 1), outer):
+        frames_on(k)
     for p in range(HALVES):
-        my_copy(z, p).start()
-
-    for k in range(outer):
+        project(0, po, p)
+
+    def pass_on(k):
         zo = goal(k)
-        total = fs[block(zo, y), :].astype(F32)
-        fy_copy(zo).wait_recv()
-        total += fy[zrows(zo), :].astype(F32)
-        if k < outer - 1:
-            fa[zrows(zo), :] = total.astype(BF)
-            fz_copy(zo).start()
-        else:
-            fr[...] = total
-
-    def pass_on(p):
-        for k in range(outer - 1):
-            zo = goal(k)
+        for p in range(HALVES):
             my_copy(zo, p).wait_recv()
-            ma[zrows(zo), cols_of(p)] = (
-                po[zrows(zo), cols_of(p)].astype(F32) + my[zrows(zo), cols_of(p)].astype(F32)
-            ).astype(BF)
+            here = (zrows(zo), cols_of(p))
+            ma[here] = (po[here].astype(F32) + my[here].astype(F32)).astype(BF)
             mz_copy(zo, p).start()
 
     def finish_frames():
@@ -432,18 +474,19 @@
         for t in range(steps):
             wave_ref[:, t, :] = samples[t * sessions:(t + 1) * sessions]
 
-    pass_on(0)
+    for k in range(outer - 1):
+        pass_on(k)
     finish_frames()
-    for p in range(1, HALVES):
-        pass_on(p)
     for p in range(HALVES):
         my_copy(z, p).wait_recv()
-        mine = po[zrows(z), cols_of(p)].astype(F32) + my[zrows(z), cols_of(p)].astype(F32)
-        for d in range(outer - 1):
+        mine[...] = po[zrows(z), cols_of(p)].astype(F32) + my[zrows(z), cols_of(p)].astype(F32)
+
+        for d in range(1, outer):
             mz_got(d, p).wait_recv()
-            mine += mz[zrows(d), cols_of(p)].astype(F32)
+            mine[...] += mz[zrows(d), cols_of(p)].astype(F32)
+
         for t in range(steps):
-            moe_ref[:, t, p * part_cols:(p + 1) * part_cols] = mine[t * sessions:(t + 1) * sessions].astype(BF)
+            moe_ref[:, t, p * part_cols:(p + 1) * part_cols] = mine[t * sessions:(t + 1) * sessions, :].astype(BF)
 
     for give in gives:
         give.wait_send()
@@ -480,7 +523,7 @@
     outer = n_e // INNER
     sessions, steps, width = args[0].shape
     rows = sessions * steps
-    used = 2 * experts + 2 * books + 2
+    used = 2 * experts + 8 + 2 * books
     lanes = used + -used % LANES
     local, _, units = w_gate.shape
     ff = 2 * units
@@ -497,14 +540,15 @@
         vm((local * ff, width), BF),
         vm(table.shape, BF),
         vm((wave_rows, table.shape[0]), BF),
-        vm((col_rows, local * ff), BF),
+        vm((wave_rows, local * ff), BF),
         vm((rows, channels), F32),
         vm((wave_rows, LANES), F32),
         vm((col_rows, width), BF),
         vm((col_rows, width), BF),
         vm((col_rows, width), BF),
         vm((col_rows, width), BF),
-        vm((hops * rows, width), BF),
+        vm((outer * rows, width), BF),
+        vm((rows, width // HALVES), F32),
         vm((wave_rows, channels), BF),
         vm((col_rows, channels), BF),
         vm((col_rows, channels), BF),
@@ -513,8 +557,9 @@
         dma(len(args)), dma(3 * local + 1), dma(3 * local), dma(3 * local),
         dma(outer * HALVES), dma(outer * HALVES), dma(outer * HALVES), dma(n_e * HALVES),
         dma(n_e - 1), dma(n_e - 1),
-        dma(outer * HALVES), dma(outer * HALVES), dma(hops * HALVES), dma(hops * HALVES),
+        dma(outer * HALVES), dma(outer * HALVES), dma(outer * HALVES), dma(outer * HALVES),
         dma(outer), dma(outer), dma(hops), dma(hops),
+        pltpu.SemaphoreType.REGULAR, pltpu.SemaphoreType.REGULAR, pltpu.SemaphoreType.REGULAR,
     ]
     any_spec = pl.BlockSpec(memory_space=pl.ANY)
     vm_spec = pl.BlockSpec(memory_space=pltpu.VMEM)

time: 47.4 us -> 43.4 us (0.916)
  Pallas kernels: 46.6 us -> 42.6 us
    pallas_call x1, Pallas kernels: 44.8 us -> 40.8 us  [exchange(): pl.pallas_call(functools.partial(kernel, n_e, experts, books), out_shape=...]
where the time goes in v1:
time: 43.4 us; the launch traced here: 43.2 us
  Pallas kernels  42.6 us (98%)
  between operations  0.64 us (1%)
    pallas_call x1, Pallas kernels, exchange(): pl.pallas_call(functools.partial(kernel, n_e, experts, books), out_shape=...  40.8 us
    pallas_call x1, Pallas kernels, per_device(): pl.pallas_call(hand_over, out_shape=tuple((jax.ShapeDtypeStruct(r.shape,...  1.74 us

profile of v1, /device:TPU:0, one launch (start us, length us, event | category | flops | bytes accessed | tf_op | source)
XLA Modules:
  0.0 43.2 jit_solution(9628220198073389597)
XLA Ops:
  0.6 40.8 %shard_map.148 = (bf16[16,2,2048]{2,1,0:T(2,128)(2,1)}, bf16[16,2,512]{2,1,0:T(2,128)(2,1)}, bf16[6,16,1024]{2,1,0:T(8,128)(2,1)}) custom-call(bf16[16,2,2048]{2,1,0:T(2,128)(2,1)} %h_ref.1, s32[2,8,16]{2,1,0:T(8,128)} %bitcast.11, f32[2,8,16]{2,1,0:T(8,128)} %bitcast.12, s32[16,2,16]{2,1,0:T(2,128)} %co_ref.1, s32[1,16]{1,0:T(1,128)} %bitcast.14, ...), custom_call_target="tpu_custom_call" | custom-call | tf_op jit(solution)/shard_map/pallas_call | solution.py:566
  41.5 1.7 %shard_map.149 = (bf16[16,2,2048]{2,1,0:T(2,128)(2,1)}, bf16[16,2,512]{2,1,0:T(2,128)(2,1)}, bf16[6,16,1024]{2,1,0:T(8,128)(2,1)}) custom-call(bf16[16,2,2048]{2,1,0:T(2,128)(2,1)} %get-tuple-element.9.a_ref, bf16[16,2,512]{2,1,0:T(2,128)(2,1)} %get-tuple-element.10.b_ref, bf16[6,16,1024]{2,1,0:T(8,128)(2,1)} %get-tuple-element.11.c_ref), custom_call_target="tpu_custom_call" | custom-call | tf_op jit(solution)/shard_map/pallas_call | solution.py:599

commit v2 on v1

--- a/solution.py
+++ b/solution.py
@@ -27,9 +27,9 @@
     moe_ref, wave_ref, new_ref,
     hv, idv, rwv, cov, owv, stv, tapv, biasv, usv,
     xg, meta, wgu, wdv, tabv, mem, act, early, told, po, pn, my, ma, mz, mine,
-    fs, fy, fa, fz, fr,
+    fs, fy, fa, fz, gz, ga, gy, fr,
     in_sem, w_sem, pws, pwr, zus, zds, yss, agr, mes, mer,
-    mys, myr, mzs, mzr, fys, fyr, fzs, fzr, below, above, aside,
+    mys, myr, mzs, mzr, fys, fyr, fzs, fzr, gzs, gzr, gys, below, above, aside,
 ):
     outer = n_e // INNER
     sessions, steps, width = hv.shape
@@ -336,8 +336,15 @@
     def hop(zo):
         return (zo - z + outer) % outer - 1
 
+    split = channels // 2
+    first_half = pl.ds(0, split)
+    second_half = pl.ds(split, split)
+
+    def pair(zo):
+        return pl.ds(pl.multiple_of(zo * INNER * rows, INNER * rows), INNER * rows)
+
     def fy_copy(zo):
-        return remote(fs.at[block(zo, 1 - y), :], fy.at[zrows(zo), :], fys.at[zo], fyr.at[zo], ye, w)
+        return remote(fs.at[block(zo, 1 - y), first_half], fy.at[zrows(zo), :], fys.at[zo], fyr.at[zo], ye, w)
 
     def fz_copy(zo):
         d = hop(zo)
@@ -346,6 +353,17 @@
     def fz_got(d):
         s = fz.at[zrows(d), :]
         return remote(s, s, fzs.at[d], fzr.at[d], ye, w)
+
+    def gz_copy(zo):
+        d = hop(zo)
+        return remote(fs.at[pair(zo), second_half], gz.at[pair(d), :], gzs.at[d], gzr.at[d], zo * INNER + y, w)
+
+    def gz_got(d):
+        s = gz.at[pair(d), :]
+        return remote(s, s, gzs.at[d], gzr.at[d], ye, w)
+
+    def gy_copy():
+        return remote(ga, gy, gys.at[0], gys.at[1], ye, w)
 
     part_cols = width // HALVES
 
@@ -407,14 +425,14 @@
 
     def frames_on(k):
         zo = goal(k)
-        total = fs[block(zo, y), :].astype(F32)
+        total = fs[block(zo, y), first_half].astype(F32)
         fy_copy(zo).wait_recv()
         total += fy[zrows(zo), :].astype(F32)
         if k < outer - 1:
             fa[zrows(zo), :] = total.astype(BF)
             fz_copy(zo).start()
         else:
-            fr[...] = total
+            fr[:, first_half] = total
 
     before()
     for step in range(1, outer):
@@ -423,17 +441,23 @@
             learn()
         if step == min(2, outer - 1):
             embed()
+    for k in range(outer - 1):
+        gz_copy(goal(k)).start()
     for k in range(outer):
         fy_copy(goal(k)).start()
 
-    for j in range(local):
+    def both_ready(j):
         ready(2 * j)
         ready(2 * j + 1)
-        hidden(0, j)
+
+    both_ready(0)
+    hidden(0, 0)
     for zo in range(outer):
         for p in range(HALVES):
             arrived(1, zo, p)
     for j in range(local):
+        if j > 0:
+            both_ready(j)
         hidden(1, j)
         if j < outer - 1:
             frames_on(j)
@@ -442,13 +466,27 @@
     for p in range(HALVES):
         project(1, pn, p)
         my_copy(goal(0), p).start()
-    for k in range(1, outer):
+    for k in range(1, outer - 1):
         for p in range(HALVES):
             my_copy(goal(k), p).start()
     for k in range(min(local, outer - 1), outer):
         frames_on(k)
+    for j in range(1, local):
+        hidden(0, j)
     for p in range(HALVES):
         project(0, po, p)
+
+    def frames_across():
+        there = fs[block(z, 1 - y), second_half].astype(F32)
+        here = fs[block(z, y), second_half].astype(F32)
+        for d in range(outer - 1):
+            gz_got(d).wait_recv()
+            start = pl.multiple_of(d * INNER * rows, rows)
+            there += gz[pl.ds(start + (1 - y) * rows, rows), :].astype(F32)
+            here += gz[pl.ds(start + y * rows, rows), :].astype(F32)
+        ga[...] = there.astype(BF)
+        gy_copy().start()
+        fr[:, second_half] = here
 
     def pass_on(k):
         zo = goal(k)
@@ -461,7 +499,9 @@
     def finish_frames():
         for d in range(outer - 1):
             fz_got(d).wait_recv()
-            fr[...] += fz[zrows(d), :].astype(F32)
+            fr[:, first_half] += fz[zrows(d), :].astype(F32)
+        gy_copy().wait_recv()
+        fr[:, second_half] += gy[...].astype(F32)
         got = [fr[t * sessions:(t + 1) * sessions, :] for t in range(steps)]
         decoded = []
         for t in range(steps):
@@ -474,7 +514,11 @@
         for t in range(steps):
             wave_ref[:, t, :] = samples[t * sessions:(t + 1) * sessions]
 
-    for k in range(outer - 1):
+    pass_on(0)
+    frames_across()
+    for p in range(HALVES):
+        my_copy(z, p).start()
+    for k in range(1, outer - 1):
         pass_on(k)
     finish_frames()
     for p in range(HALVES):
@@ -488,6 +532,7 @@
         for t in range(steps):
             moe_ref[:, t, p * part_cols:(p + 1) * part_cols] = mine[t * sessions:(t + 1) * sessions, :].astype(BF)
 
+    gy_copy().wait_send()
     for give in gives:
         give.wait_send()
     for d in range(1, n_e):
@@ -508,6 +553,7 @@
     for k in range(outer - 1):
         zo = goal(k)
         fz_copy(zo).wait_send()
+        gz_copy(zo).wait_send()
         for p in range(HALVES):
             mz_copy(zo, p).wait_send()
 
@@ -550,15 +596,18 @@
         vm((outer * rows, width), BF),
         vm((rows, width // HALVES), F32),
         vm((wave_rows, channels), BF),
-        vm((col_rows, channels), BF),
-        vm((col_rows, channels), BF),
-        vm((hops * rows, channels), BF),
+        vm((col_rows, channels // 2), BF),
+        vm((col_rows, channels // 2), BF),
+        vm((hops * rows, channels // 2), BF),
+        vm((hops * INNER * rows, channels // 2), BF),
+        vm((rows, channels // 2), BF),
+        vm((rows, channels // 2), BF),
         vm((rows, channels), F32),
         dma(len(args)), dma(3 * local + 1), dma(3 * local), dma(3 * local),
         dma(outer * HALVES), dma(outer * HALVES), dma(outer * HALVES), dma(n_e * HALVES),
         dma(n_e - 1), dma(n_e - 1),
         dma(outer * HALVES), dma(outer * HALVES), dma(outer * HALVES), dma(outer * HALVES),
-        dma(outer), dma(outer), dma(hops), dma(hops),
+        dma(outer), dma(outer), dma(hops), dma(hops), dma(hops), dma(hops), dma(2),
         pltpu.SemaphoreType.REGULAR, pltpu.SemaphoreType.REGULAR, pltpu.SemaphoreType.REGULAR,
     ]
     any_spec = pl.BlockSpec(memory_space=pl.ANY)

time: 43.4 us -> 41.4 us (0.954)
  Pallas kernels: 42.6 us -> 40.6 us
    pallas_call x1, Pallas kernels: 40.8 us -> 38.8 us  [exchange(): pl.pallas_call(functools.partial(kernel, n_e, experts, books), out_shape=...]
where the time goes in v2:
time: 41.4 us; the launch traced here: 41.2 us
  Pallas kernels  40.6 us (98%)
  between operations  0.64 us (2%)
    pallas_call x1, Pallas kernels, exchange(): pl.pallas_call(functools.partial(kernel, n_e, experts, books), out_shape=...  38.8 us
    pallas_call x1, Pallas kernels, per_device(): pl.pallas_call(hand_over, out_shape=tuple((jax.ShapeDtypeStruct(r.shape,...  1.74 us

profile of v2, /device:TPU:0, one launch (start us, length us, event | category | flops | bytes accessed | tf_op | source)
XLA Modules:
  0.0 41.2 jit_solution(7780978708103518555)
XLA Ops:
  0.6 38.8 %shard_map.148 = (bf16[16,2,2048]{2,1,0:T(2,128)(2,1)}, bf16[16,2,512]{2,1,0:T(2,128)(2,1)}, bf16[6,16,1024]{2,1,0:T(8,128)(2,1)}) custom-call(bf16[16,2,2048]{2,1,0:T(2,128)(2,1)} %h_ref.1, s32[2,8,16]{2,1,0:T(8,128)} %bitcast.11, f32[2,8,16]{2,1,0:T(8,128)} %bitcast.12, s32[16,2,16]{2,1,0:T(2,128)} %co_ref.1, s32[1,16]{1,0:T(1,128)} %bitcast.14, ...), custom_call_target="tpu_custom_call" | custom-call | tf_op jit(solution)/shard_map/pallas_call | solution.py:615
  39.5 1.7 %shard_map.149 = (bf16[16,2,2048]{2,1,0:T(2,128)(2,1)}, bf16[16,2,512]{2,1,0:T(2,128)(2,1)}, bf16[6,16,1024]{2,1,0:T(8,128)(2,1)}) custom-call(bf16[16,2,2048]{2,1,0:T(2,128)(2,1)} %get-tuple-element.9.a_ref, bf16[16,2,512]{2,1,0:T(2,128)(2,1)} %get-tuple-element.10.b_ref, bf16[6,16,1024]{2,1,0:T(8,128)(2,1)} %get-tuple-element.11.c_ref), custom_call_target="tpu_custom_call" | custom-call | tf_op jit(solution)/shard_map/pallas_call | solution.py:648

commit v3 on v2

--- a/solution.py
+++ b/solution.py
@@ -558,10 +558,15 @@
             mz_copy(zo, p).wait_send()
 
 
-def hand_over(a_ref, b_ref, c_ref, a_out, b_out, c_out):
-    a_out[...] = a_ref[...]
-    b_out[...] = b_ref[...]
-    c_out[...] = c_ref[...]
+def hand_over(a_ref, b_ref, c_ref, a_out, b_out, c_out, sems):
+    copies = [
+        pltpu.make_async_copy(src, dst, sems.at[i])
+        for i, (src, dst) in enumerate(((a_ref, a_out), (b_ref, b_out), (c_ref, c_out)))
+    ]
+    for copy in copies:
+        copy.start()
+    for copy in copies:
+        copy.wait()
 
 
 def exchange(args, w_gate, w_up, w_down, table, experts, books):
@@ -615,9 +620,9 @@
     return pl.pallas_call(
         functools.partial(kernel, n_e, experts, books),
         out_shape=(
-            jax.ShapeDtypeStruct((sessions, steps, width), BF),
-            jax.ShapeDtypeStruct((sessions, steps, args[8].shape[1]), BF),
-            jax.ShapeDtypeStruct(args[5].shape, BF),
+            vm((sessions, steps, width), BF),
+            vm((sessions, steps, args[8].shape[1]), BF),
+            vm(args[5].shape, BF),
         ),
         in_specs=[any_spec] * (len(args) + 4),
         out_specs=(vm_spec, vm_spec, vm_spec),
@@ -649,8 +654,9 @@
         hand_over,
         out_shape=tuple(jax.ShapeDtypeStruct(r.shape, r.dtype) for r in results),
         in_specs=[vm_spec] * 3,
-        out_specs=(vm_spec,) * 3,
-    )(*results)
+        out_specs=(pl.BlockSpec(memory_space=pl.ANY),) * 3,
+        scratch_shapes=[pltpu.SemaphoreType.DMA((3,))],
+    )(*[pltpu.with_memory_space_constraint(r, pltpu.VMEM) for r in results])
     return moe, samples, carried.transpose(1, 0, 2)
 
 

time: 41.4 us -> 39.7 us (0.959)
  Pallas kernels: 40.6 us -> 38.9 us
    pallas_call x1, Pallas kernels: 1.74 us -> 0.76 us  [per_device(): pl.pallas_call(hand_over, out_shape=tuple((jax.ShapeDtypeStruct(r.shape,...]
    pallas_call x1, Pallas kernels: 38.8 us -> 38.1 us  [exchange(): pl.pallas_call(functools.partial(kernel, n_e, experts, books), out_shape=...]
where the time goes in v3:
time: 39.7 us; the launch traced here: 39.5 us
  Pallas kernels  38.9 us (98%)
  between operations  0.64 us (2%)
    pallas_call x1, Pallas kernels, exchange(): pl.pallas_call(functools.partial(kernel, n_e, experts, books), out_shape=...  38.1 us

profile of v3, /device:TPU:0, one launch (start us, length us, event | category | flops | bytes accessed | tf_op | source)
XLA Modules:
  0.0 39.5 jit_solution(10625093466114308278)
XLA Ops:
  0.6 38.1 %shard_map.148 = (bf16[16,2,2048]{2,1,0:T(2,128)(2,1)S(1)}, bf16[16,2,512]{2,1,0:T(2,128)(2,1)S(1)}, bf16[6,16,1024]{2,1,0:T(8,128)(2,1)S(1)}) custom-call(bf16[16,2,2048]{2,1,0:T(2,128)(2,1)} %h_ref.1, s32[2,8,16]{2,1,0:T(8,128)} %bitcast.11, f32[2,8,16]{2,1,0:T(8,128)} %bitcast.12, s32[16,2,16]{2,1,0:T(2,128)} %co_ref.1, s32[1,16]{1,0:T(1,128)} %bitcast.14, ...), custom_call_target="tpu_custom_call" | custom-call | tf_op jit(solution)/shard_map/pallas_call | solution.py:620
  38.8 0.8 %shard_map.149 = (bf16[16,2,2048]{2,1,0:T(2,128)(2,1)}, bf16[16,2,512]{2,1,0:T(2,128)(2,1)}, bf16[6,16,1024]{2,1,0:T(8,128)(2,1)}) custom-call(bf16[16,2,2048]{2,1,0:T(2,128)(2,1)S(1)} %get-tuple-element.9.a_ref, bf16[16,2,512]{2,1,0:T(2,128)(2,1)S(1)} %get-tuple-element.10.b_ref, bf16[6,16,1024]{2,1,0:T(8,128)(2,1)S(1)} %get-tuple-element.11.c_ref), custom_call_target="tpu_custom_call" | custom-call | tf_op jit(solution)/shard_map/pallas_call | solution.py:653

commit v4 on v3

--- a/solution.py
+++ b/solution.py
@@ -14,6 +14,7 @@
 LANES = 128
 INNER = 2
 HALVES = 2
+PIECES = 2
 
 
 def dot(a, b):
@@ -26,7 +27,7 @@
     wg_ref, wu_ref, wd_ref, tab_ref,
     moe_ref, wave_ref, new_ref,
     hv, idv, rwv, cov, owv, stv, tapv, biasv, usv,
-    xg, meta, wgu, wdv, tabv, mem, act, early, told, po, pn, my, ma, mz, mine,
+    xg, meta, wgu, wdv, tabv, mem, act, acc, early, told, po, pn, my, ma, mz, mine,
     fs, fy, fa, fz, gz, ga, gy, fr,
     in_sem, w_sem, pws, pwr, zus, zds, yss, agr, mes, mer,
     mys, myr, mzs, mzr, fys, fyr, fzs, fzr, gzs, gzr, gys, below, above, aside,
@@ -109,29 +110,31 @@
         remote(src, dst, pws.at[i], pwr.at[i], e, peer) for i, (src, dst) in enumerate(weights(peer))
     ]
 
-    half = rows // HALVES
+    piece_cols = width // PIECES
 
     def at(rel, zo, p):
-        return pl.ds(pl.multiple_of((rel * outer + zo) * rows + p * half, half), half)
+        return (
+            pl.ds(pl.multiple_of((rel * outer + zo) * rows, rows), rows), pl.ds(p * piece_cols, piece_cols)
+        )
 
     def agsem(rel, zo, p):
-        return agr.at[(rel * outer + zo) * HALVES + p]
+        return agr.at[(rel * outer + zo) * PIECES + p]
 
     def up(zo, p):
-        s = xg.at[at(0, zo, p), :]
-        return remote(s, s, zus.at[zo * HALVES + p], agsem(0, zo, p), (z + 1) * INNER + y, w)
+        s = xg.at[at(0, zo, p)]
+        return remote(s, s, zus.at[zo * PIECES + p], agsem(0, zo, p), (z + 1) * INNER + y, w)
 
     def down(zo, p):
-        s = xg.at[at(0, zo, p), :]
-        return remote(s, s, zds.at[zo * HALVES + p], agsem(0, zo, p), (z - 1) * INNER + y, w)
+        s = xg.at[at(0, zo, p)]
+        return remote(s, s, zds.at[zo * PIECES + p], agsem(0, zo, p), (z - 1) * INNER + y, w)
 
     def across(zo, p):
         return remote(
-            xg.at[at(0, zo, p), :], xg.at[at(1, zo, p), :], yss.at[zo * HALVES + p], agsem(1, zo, p), ye, w
+            xg.at[at(0, zo, p)], xg.at[at(1, zo, p)], yss.at[zo * PIECES + p], agsem(1, zo, p), ye, w
         )
 
     def arrived(rel, zo, p):
-        s = xg.at[at(rel, zo, p), :]
+        s = xg.at[at(rel, zo, p)]
         remote(s, s, yss.at[0], agsem(rel, zo, p), ye, w).wait_recv()
 
     def meta_at(te, se):
@@ -161,7 +164,7 @@
         load.start()
     pl.semaphore_wait(barrier, 2 + (z > 0).astype(jnp.int32) + (z < outer - 1).astype(jnp.int32))
 
-    for p in range(HALVES):
+    for p in range(PIECES):
         @pl.when(z + 1 < outer)
         def _():
             up(z, p).start()
@@ -260,7 +263,7 @@
             new_ref[i] = stv[i + steps]
 
     def forward(step):
-        for p in range(HALVES):
+        for p in range(PIECES):
             @pl.when(z - step >= 0)
             def _():
                 zo = z - step
@@ -388,6 +391,7 @@
         return remote(s, s, mzs.at[0], mzr.at[there * HALVES + p], ye, w)
 
     rc = min(col_rows, 128)
+    early_cols = width - piece_cols
 
     def looped(count, body):
         if count == 1:
@@ -413,6 +417,33 @@
 
         looped(col_rows // rc, piece)
 
+    def hidden_start(j):
+        def piece(i):
+            here = pl.ds(pl.multiple_of(col_rows + i * rc, rc), rc)
+            there = pl.ds(pl.multiple_of(i * rc, rc), rc)
+            x = xg[here, :early_cols]
+            tile = 2 * ff // 3 if ff % (3 * LANES) == 0 else ff
+            for n in range(0, 2 * ff, tile):
+                acc[there, j * 2 * ff + n:j * 2 * ff + n + tile] = dot(x, wgu[j, :early_cols, n:n + tile])
+
+        looped(col_rows // rc, piece)
+
+    def hidden_end(j):
+        def piece(i):
+            here = pl.ds(pl.multiple_of(col_rows + i * rc, rc), rc)
+            there = pl.ds(pl.multiple_of(i * rc, rc), rc)
+            x = xg[here, early_cols:]
+            weight = told[here, books + 1 + j:books + 2 + j]
+            tile = ff // 3 if ff % (3 * LANES) == 0 else ff
+            for n in range(0, ff, tile):
+                base = j * 2 * ff + n
+                g = acc[there, base:base + tile] + dot(x, wgu[j, early_cols:, n:n + tile])
+                u = acc[there, base + ff:base + ff + tile] + dot(x, wgu[j, early_cols:, ff + n:ff + n + tile])
+                a = g / (1.0 + jnp.exp(-g)) * u * weight
+                act[here, j * ff + n:j * ff + n + tile] = a.astype(BF)
+
+        looped(col_rows // rc, piece)
+
     def project(rel, dst, p):
         def piece(i):
             here = pl.ds(pl.multiple_of(rel * col_rows + i * rc, rc), rc)
@@ -453,12 +484,16 @@
     both_ready(0)
     hidden(0, 0)
     for zo in range(outer):
-        for p in range(HALVES):
+        for p in range(PIECES - 1):
             arrived(1, zo, p)
     for j in range(local):
         if j > 0:
             both_ready(j)
-        hidden(1, j)
+        hidden_start(j)
+    for zo in range(outer):
+        arrived(1, zo, PIECES - 1)
+    for j in range(local):
+        hidden_end(j)
         if j < outer - 1:
             frames_on(j)
     for j in range(local):
@@ -538,7 +573,7 @@
     for d in range(1, n_e):
         tell(d).wait_send()
     for zo in range(outer):
-        for p in range(HALVES):
+        for p in range(PIECES):
             @pl.when((z + 1 < outer) & (zo <= z))
             def _():
                 up(zo, p).wait_send()
@@ -548,6 +583,7 @@
                 down(zo, p).wait_send()
 
             across(zo, p).wait_send()
+        for p in range(HALVES):
             my_copy(zo, p).wait_send()
         fy_copy(zo).wait_send()
     for k in range(outer - 1):
@@ -592,6 +628,7 @@
         vm(table.shape, BF),
         vm((wave_rows, table.shape[0]), BF),
         vm((wave_rows, local * ff), BF),
+        vm((col_rows, local * 2 * ff), F32),
         vm((rows, channels), F32),
         vm((wave_rows, LANES), F32),
         vm((col_rows, width), BF),
@@ -609,7 +646,7 @@
         vm((rows, channels // 2), BF),
         vm((rows, channels), F32),
         dma(len(args)), dma(3 * local + 1), dma(3 * local), dma(3 * local),
-        dma(outer * HALVES), dma(outer * HALVES), dma(outer * HALVES), dma(n_e * HALVES),
+        dma(outer * PIECES), dma(outer * PIECES), dma(outer * PIECES), dma(n_e * PIECES),
         dma(n_e - 1), dma(n_e - 1),
         dma(outer * HALVES), dma(outer * HALVES), dma(outer * HALVES), dma(outer * HALVES),
         dma(outer), dma(outer), dma(hops), dma(hops), dma(hops), dma(hops), dma(2),

time: 39.7 us -> 39 us (0.982)
  Pallas kernels: 38.9 us -> 38.2 us
    pallas_call x1, Pallas kernels: 38.1 us -> 37.5 us  [exchange(): pl.pallas_call(functools.partial(kernel, n_e, experts, books), out_shape=...]
where the time goes in v4:
time: 39 us; the launch traced here: 38.9 us
  Pallas kernels  38.2 us (98%)
  between operations  0.64 us (2%)
    pallas_call x1, Pallas kernels, exchange(): pl.pallas_call(functools.partial(kernel, n_e, experts, books), out_shape=...  37.5 us

profile of v4, /device:TPU:0, one launch (start us, length us, event | category | flops | bytes accessed | tf_op | source)
XLA Modules:
  0.0 38.9 jit_solution(7006373962350060509)
XLA Ops:
  0.6 37.5 %shard_map.148 = (bf16[16,2,2048]{2,1,0:T(2,128)(2,1)S(1)}, bf16[16,2,512]{2,1,0:T(2,128)(2,1)S(1)}, bf16[6,16,1024]{2,1,0:T(8,128)(2,1)S(1)}) custom-call(bf16[16,2,2048]{2,1,0:T(2,128)(2,1)} %h_ref.1, s32[2,8,16]{2,1,0:T(8,128)} %bitcast.11, f32[2,8,16]{2,1,0:T(8,128)} %bitcast.12, s32[16,2,16]{2,1,0:T(2,128)} %co_ref.1, s32[1,16]{1,0:T(1,128)} %bitcast.14, ...), custom_call_target="tpu_custom_call" | custom-call | tf_op jit(solution)/shard_map/pallas_call | solution.py:657
  38.1 0.8 %shard_map.149 = (bf16[16,2,2048]{2,1,0:T(2,128)(2,1)}, bf16[16,2,512]{2,1,0:T(2,128)(2,1)}, bf16[6,16,1024]{2,1,0:T(8,128)(2,1)}) custom-call(bf16[16,2,2048]{2,1,0:T(2,128)(2,1)S(1)} %get-tuple-element.9.a_ref, bf16[16,2,512]{2,1,0:T(2,128)(2,1)S(1)} %get-tuple-element.10.b_ref, bf16[6,16,1024]{2,1,0:T(8,128)(2,1)S(1)} %get-tuple-element.11.c_ref), custom_call_target="tpu_custom_call" | custom-call | tf_op jit(solution)/shard_map/pallas_call | solution.py:690

commit v5 on v4

--- a/solution.py
+++ b/solution.py
@@ -468,7 +468,7 @@
     before()
     for step in range(1, outer):
         forward(step)
-        if step == 1:
+        if step == min(2, outer - 1):
             learn()
         if step == min(2, outer - 1):
             embed()

time: 39 us -> 39 us (level)
  no operation moved by 1% of the time
where the time goes in v5:
time: 39 us; the launch traced here: 38.9 us
  Pallas kernels  38.2 us (98%)
  between operations  0.64 us (2%)
    pallas_call x1, Pallas kernels, exchange(): pl.pallas_call(functools.partial(kernel, n_e, experts, books), out_shape=...  37.5 us

profile of v5, /device:TPU:0, one launch (start us, length us, event | category | flops | bytes accessed | tf_op | source)
XLA Modules:
  0.0 38.9 jit_solution(9083281816671004645)
XLA Ops:
  0.6 37.5 %shard_map.148 = (bf16[16,2,2048]{2,1,0:T(2,128)(2,1)S(1)}, bf16[16,2,512]{2,1,0:T(2,128)(2,1)S(1)}, bf16[6,16,1024]{2,1,0:T(8,128)(2,1)S(1)}) custom-call(bf16[16,2,2048]{2,1,0:T(2,128)(2,1)} %h_ref.1, s32[2,8,16]{2,1,0:T(8,128)} %bitcast.11, f32[2,8,16]{2,1,0:T(8,128)} %bitcast.12, s32[16,2,16]{2,1,0:T(2,128)} %co_ref.1, s32[1,16]{1,0:T(1,128)} %bitcast.14, ...), custom_call_target="tpu_custom_call" | custom-call | tf_op jit(solution)/shard_map/pallas_call | solution.py:657
  38.1 0.8 %shard_map.149 = (bf16[16,2,2048]{2,1,0:T(2,128)(2,1)}, bf16[16,2,512]{2,1,0:T(2,128)(2,1)}, bf16[6,16,1024]{2,1,0:T(8,128)(2,1)}) custom-call(bf16[16,2,2048]{2,1,0:T(2,128)(2,1)S(1)} %get-tuple-element.9.a_ref, bf16[16,2,512]{2,1,0:T(2,128)(2,1)S(1)} %get-tuple-element.10.b_ref, bf16[6,16,1024]{2,1,0:T(8,128)(2,1)S(1)} %get-tuple-element.11.c_ref), custom_call_target="tpu_custom_call" | custom-call | tf_op jit(solution)/shard_map/pallas_call | solution.py:690
